TPU v7x, 256 devices: a whole 4x4x8 slice. The times are simulated.
256 devices in a mesh: dp: 32 (over z, y), section: 2 (over core), tensor: 4 (over x).
Axes of the slice: x: 4, y: 4, z: 8, core: 2. Of those that a mesh axis runs over, the one named last changes fastest.
Arguments:
- tokens: bfloat16 [8192, 2048], P('dp'), may hold values from -6 to 6
- base_rows: int32 [128], replicated, may hold values from 1 to 6, as said below
- baseline_owner: int32 [128], replicated, may hold values from 0 to 31, as said below
- cotangent: bfloat16 [2, 16384, 2048], P('section', 'dp'), may hold values from -6 to 6
- pre_gain: float32 [2, 2048], P('section'), may hold values from 0.25 to 1.75
- input_proj: bfloat16 [2, 2048, 2048], P('section', None, 'tensor'), may hold values from -0.125 to 0.125
- gate_proj: bfloat16 [2, 2048, 2048], P('section', None, 'tensor'), may hold values from -0.125 to 0.125
- state_proj: bfloat16 [2, 2048, 256], P('section'), may hold values from -0.125 to 0.125
- step_proj: bfloat16 [2, 2048, 32], P('section', None, 'tensor'), may hold values from -0.125 to 0.125
- step_bias: float32 [2, 32], P('section', 'tensor'), may hold values from -6 to -1.5
- decay_log: float32 [2, 32], P('section', 'tensor'), may hold values from 0 to 2.5
- skip_gain: float32 [2, 32], P('section', 'tensor'), may hold values from 0.5 to 1.5
- norm_gain: float32 [2, 2048], P('section', 'tensor'), may hold values from 0.25 to 1.75
- out_proj: bfloat16 [2, 2048, 2048], P('section', 'tensor'), may hold values from -0.125 to 0.125
Outputs:
- activations: bfloat16 [2, 16384, 2048], P('section', 'dp')
- out_grad: bfloat16 [2, 2048, 2048], P('section', 'tensor', 'dp')
Inputs may be any that keep to these rules, and one draw needn't show every extreme that they name: `base_rows`: over all baselines they sum to 256; some baseline has exactly 6. `baseline_owner`: every owner holds exactly 4 baselines; the base_rows of one owner's baselines sum to at most 16, and for some owner to exactly 16.
All inputs are finite; a program needn't handle non-finite values.
Results may differ from a plain program's by a relative error of at most 0.025.
Values may be sent and summed in bfloat16 or wider, within the bound.
A program may use at most 128 MiB of HBM per device.

v0:
```python
import jax
import jax.numpy as jnp
from jax import lax
from jax.sharding import PartitionSpec as P

HEADS = 32
HEADDIM = 64
NSTATE = 128
BLOCK = 64
MICRO = 2
EPS = 1e-05


def from_behind(value, axis, steps):
    count = lax.axis_size(axis)
    first, last = (max(0, -steps), min(count, count - steps))
    return lax.ppermute(value, axis, [(source, source + steps) for source in range(first, last)])


def layout_tables(base_rows, baseline_owner):
    count = base_rows.shape[0]
    index = jnp.arange(count, dtype=jnp.int32)
    ends = jnp.cumsum(base_rows)
    starts = ends - base_rows
    earlier = (baseline_owner[:, None] == baseline_owner[None, :]) & (
        index[None, :] < index[:, None]
    )
    owner_start = jnp.sum(jnp.where(earlier, base_rows[None, :], 0), axis=1)
    return (index, starts, ends, owner_start)


def block_scan(
    heads_in, b_rows, c_rows, step_size, decay_rate, segment, state, prev_segment, block
):
    total_rows, head_count, head_dim = heads_in.shape
    blocks = total_rows // block

    def advance(carried_in, item):
        state_now, segment_before = carried_in
        x_blk, b_blk, c_blk, dt_blk, seg_blk = item
        running = jnp.cumsum(dt_blk * decay_rate[None, :], axis=0)
        positions = jnp.arange(block, dtype=jnp.int32)
        together = (seg_blk[:, None] == seg_blk[None, :]) & (
            positions[:, None] >= positions[None, :]
        )
        spread = jnp.minimum(running[:, None, :] - running[None, :, :], 0.0)
        decay_mask = jnp.where(together[:, :, None], jnp.exp(spread), 0.0)
        scores = jnp.dot(c_blk, b_blk.T, preferred_element_type=jnp.float32)
        weights = (decay_mask * scores[:, :, None] * dt_blk[None, :, :]).astype(jnp.bfloat16)
        within = jnp.einsum("ijh,jhp->ihp", weights, x_blk, preferred_element_type=jnp.float32)
        keep_in = (seg_blk == segment_before).astype(jnp.float32)
        readout = jnp.einsum(
            "in,hpn->ihp", c_blk, state_now.astype(jnp.bfloat16), preferred_element_type=jnp.float32
        )
        from_state = keep_in[:, None, None] * jnp.exp(running)[:, :, None] * readout
        last_segment = seg_blk[-1]
        tail_weight = (
            jnp.where(
                (seg_blk == last_segment)[:, None], jnp.exp(running[-1][None, :] - running), 0.0
            )
            * dt_blk
        )
        scaled = (tail_weight[:, :, None] * x_blk.astype(jnp.float32)).astype(jnp.bfloat16)
        fresh_term = jnp.einsum("jhp,jn->hpn", scaled, b_blk, preferred_element_type=jnp.float32)
        keep_state = (last_segment == segment_before).astype(jnp.float32)
        state_next = keep_state * jnp.exp(running[-1])[:, None, None] * state_now + fresh_term
        return ((state_next, last_segment), within + from_state)

    scanned = (
        heads_in.reshape(blocks, block, head_count, head_dim),
        b_rows.reshape(blocks, block, -1),
        c_rows.reshape(blocks, block, -1),
        step_size.reshape(blocks, block, head_count),
        segment.reshape(blocks, block),
    )
    (state, prev_segment), outputs = lax.scan(advance, (state, prev_segment), scanned)
    return (outputs.reshape(total_rows, head_count, head_dim), state, prev_segment)


def block_layer(rows_in, segment, carried_state, params):
    (
        pre_gain,
        input_proj,
        gate_proj,
        state_proj,
        step_proj,
        step_bias,
        decay_log,
        skip_gain,
        norm_gain,
        out_proj,
    ) = params
    row_count = rows_in.shape[0]
    local_heads = step_proj.shape[1]
    rows_f = rows_in.astype(jnp.float32)
    normed = (
        rows_f * lax.rsqrt(jnp.mean(rows_f * rows_f, axis=-1, keepdims=True) + EPS) * pre_gain
    ).astype(jnp.bfloat16)
    scan_in = jax.nn.silu(jnp.dot(normed, input_proj, preferred_element_type=jnp.float32)).astype(
        jnp.bfloat16
    )
    gate_pre = jnp.dot(normed, gate_proj, preferred_element_type=jnp.float32)
    state_io = jax.nn.silu(jnp.dot(normed, state_proj, preferred_element_type=jnp.float32)).astype(
        jnp.bfloat16
    )
    step_size = jax.nn.softplus(
        jnp.dot(normed, step_proj, preferred_element_type=jnp.float32) + step_bias
    )
    decay_rate = -jnp.exp(decay_log)
    heads_in = scan_in.reshape(row_count, local_heads, HEADDIM)
    scan_out, state_end, segment_end = block_scan(
        heads_in,
        state_io[:, :NSTATE],
        state_io[:, NSTATE:],
        step_size,
        decay_rate,
        segment,
        carried_state[0],
        carried_state[1],
        BLOCK,
    )
    scan_out = scan_out + skip_gain[None, :, None] * heads_in.astype(jnp.float32)
    gated = scan_out.reshape(row_count, local_heads * HEADDIM) * jax.nn.silu(gate_pre)
    sq_sum = lax.psum(jnp.sum(gated * gated, axis=-1), "tensor")
    y_norm = (gated * lax.rsqrt(sq_sum[:, None] / (HEADS * HEADDIM) + EPS) * norm_gain).astype(
        jnp.bfloat16
    )
    row_share = row_count // lax.axis_size("tensor")
    summed = lax.psum_scatter(
        jnp.dot(y_norm, out_proj, preferred_element_type=jnp.float32).astype(jnp.bfloat16),
        "tensor",
        scatter_dimension=0,
        tiled=True,
    ).astype(jnp.float32)
    own_rows = lax.dynamic_slice_in_dim(rows_f, lax.axis_index("tensor") * row_share, row_share, 0)
    own_out = (own_rows + summed).astype(jnp.bfloat16)
    result = lax.all_gather(own_out, "tensor", axis=0, tiled=True)
    return (result, y_norm, (state_end, segment_end))


def grad_term(y_norm, cot_rows):
    return lax.dot_general(
        y_norm, cot_rows, (((0,), (0,)), ((), ())), preferred_element_type=jnp.float32
    )


def per_device(
    tokens,
    base_rows,
    baseline_owner,
    cotangent,
    pre_gain,
    input_proj,
    gate_proj,
    state_proj,
    step_proj,
    step_bias,
    decay_log,
    skip_gain,
    norm_gain,
    out_proj,
):
    dp_count = lax.axis_size("dp")
    tok_rows, feat_width = tokens.shape
    slot_cap = 2 * tok_rows // dp_count
    own_slots = slot_cap * dp_count
    index, starts, ends, owner_start = layout_tables(base_rows, baseline_owner)
    local = jnp.arange(tok_rows, dtype=jnp.int32)
    inside = ((starts[None, :] <= local[:, None]) & (local[:, None] < ends[None, :])).astype(
        jnp.int32
    )
    row_start = jnp.sum(inside * starts[None, :], axis=1)
    row_owner = jnp.sum(inside * baseline_owner[None, :], axis=1)
    row_ostart = jnp.sum(inside * owner_start[None, :], axis=1)
    send_slot = row_owner * slot_cap + row_ostart + local - row_start
    outgoing = (
        jnp.zeros((own_slots, feat_width), jnp.bfloat16)
        .at[send_slot]
        .set(tokens)
        .reshape(dp_count, slot_cap, feat_width)
    )
    owner_index = lax.axis_index("dp")
    place = jnp.arange(slot_cap, dtype=jnp.int32)
    held = (
        (baseline_owner[None, :] == owner_index)
        & (owner_start[None, :] <= place[:, None])
        & (place[:, None] < owner_start[None, :] + base_rows[None, :])
    ).astype(jnp.int32)
    got_start = jnp.sum(held * owner_start[None, :], axis=1)
    got_len = jnp.sum(held * base_rows[None, :], axis=1)
    got_id = jnp.sum(held * index[None, :], axis=1)
    got_any = jnp.sum(held, axis=1)
    sender = jnp.arange(dp_count, dtype=jnp.int32)[:, None]
    recv_slot = (
        dp_count * got_start[None, :]
        + sender * got_len[None, :]
        + place[None, :]
        - got_start[None, :]
    )
    recv_slot = jnp.where(got_any[None, :] > 0, recv_slot, own_slots).reshape(-1)
    id_rows = jnp.broadcast_to(got_id[None, :], (dp_count, slot_cap)).reshape(-1)
    slot_ids = jnp.full((own_slots,), -1, jnp.int32).at[recv_slot].set(id_rows, mode="drop")
    arrived = lax.all_to_all(outgoing, "dp", split_axis=0, concat_axis=0, tiled=True)
    width = arrived.shape[-1]
    stream = (
        jnp.zeros((own_slots, width), jnp.bfloat16)
        .at[recv_slot]
        .set(arrived.reshape(-1, width), mode="drop")
    )
    starts_flag = jnp.concatenate(
        [jnp.ones((1,), jnp.int32), (slot_ids[1:] != slot_ids[:-1]).astype(jnp.int32)]
    )
    segment = jnp.cumsum(starts_flag)
    section_idx = lax.axis_index("section")
    params = (
        pre_gain[0],
        input_proj[0],
        gate_proj[0],
        state_proj[0],
        step_proj[0],
        step_bias[0],
        decay_log[0],
        skip_gain[0],
        norm_gain[0],
        out_proj[0],
    )
    local_heads = step_proj.shape[2]
    micro_rows = own_slots // MICRO
    zero_state = (jnp.zeros((local_heads, HEADDIM, NSTATE), jnp.float32), jnp.array(-1, jnp.int32))
    cot_own = cotangent[0]
    carried_state = zero_state
    handed = jnp.zeros((micro_rows, feat_width), jnp.bfloat16)
    outputs_all = jnp.zeros((own_slots, feat_width), jnp.bfloat16)
    grad_acc = jnp.zeros((out_proj.shape[1], feat_width), jnp.float32)
    for turn_index in range(MICRO + 1):
        micro_index = turn_index - section_idx
        active_turn = (micro_index >= 0) & (micro_index < MICRO)
        micro_index = jnp.clip(micro_index, 0, MICRO - 1)
        first_row = micro_index * micro_rows
        own_in = lax.dynamic_slice_in_dim(stream, first_row, micro_rows, 0)
        source = jnp.where(section_idx == 0, own_in, handed)
        seg_part = lax.dynamic_slice_in_dim(segment, first_row, micro_rows, 0)
        result, y_norm, moved = block_layer(source, seg_part, carried_state, params)
        carried_state = jax.tree.map(
            lambda new_val, old_val: jnp.where(active_turn, new_val, old_val), moved, carried_state
        )
        outputs_all = jnp.where(
            active_turn,
            lax.dynamic_update_slice_in_dim(outputs_all, result, first_row, 0),
            outputs_all,
        )
        cot_part = lax.dynamic_slice_in_dim(cot_own, first_row, micro_rows, 0)
        grad_acc = grad_acc + jnp.where(active_turn, grad_term(y_norm, cot_part), 0.0)
        if turn_index < MICRO:
            handed = from_behind(result, "section", 1)
    grad_share = lax.psum_scatter(
        grad_acc.astype(jnp.bfloat16), "dp", scatter_dimension=1, tiled=True
    )
    return (outputs_all[None], grad_share[None])


def solution(mesh):
    return jax.shard_map(
        per_device,
        mesh=mesh,
        in_specs=(
            P("dp", None),
            P(),
            P(),
            P("section", "dp", None),
            P("section", None),
            P("section", None, "tensor"),
            P("section", None, "tensor"),
            P("section", None, None),
            P("section", None, "tensor"),
            P("section", "tensor"),
            P("section", "tensor"),
            P("section", "tensor"),
            P("section", "tensor"),
            P("section", "tensor", None),
        ),
        out_specs=(P("section", "dp", None), P("section", "tensor", "dp")),
        check_vma=False,
    )
```

profile of v0, /device:TPU:2, one launch (start us, length us, event | category | flops | bytes accessed | tf_op | source)
XLA Modules:
  0.0 645.6 jit_solution(3707332609720669846)
XLA Ops:
  7.2 1.0 select_reduce_fusion.3
  10.8 4.4 scatter_custom_fusion
  15.2 11.8 %all-to-all-start = ((bf16[32,16,2048]{2,1,0:T(8,128)(2,1)}), bf16[32,16,2048]{2,1,0:T(8,128)(2,1)}, u32[]{:S(2)}, u32[]{:S(2)}) async-start(bf16[32,16,2048]{2,1,0:T(8,128)(2,1)} %bitcast.297), calls=%async_computation | async-start | bytes 4194304 | tf_op jit(solution)/shard_map/all_to_all | solution.py:203
  28.2 2.4 scatter_custom_fusion.2
  32.2 44.9 %all-to-all-done = bf16[32,16,2048]{2,1,0:T(8,128)(2,1)} async-done(((bf16[32,16,2048]{2,1,0:T(8,128)(2,1)}), bf16[32,16,2048]{2,1,0:T(8,128)(2,1)}, u32[]{:S(2)}, u32[]{:S(2)}) %all-to-all-start) | async-done | bytes 2097184 | tf_op jit(solution)/shard_map/all_to_all | solution.py:203
  77.1 6.1 scatter_custom_fusion.1
  83.2 1.6 multiply_reduce_fusion.2
  84.9 1.7 compare_select_fusion.2
  87.4 2.2 multiply_convert_fusion.20
  91.4 1.1 broadcast.415.clone2
  92.4 33.7 %while.45 = (s32[]{:T(128)}, f32[8,64,128]{2,1,0:T(8,128)S(1)}, s32[]{:T(128)}, f32[4,64,8,64]{3,2,1,0:T(8,128)}, s32[4,64]{1,0:T(4,128)S(1)}, /*index=5*/f32[4,...) while((s32[]{:T(128)}, f32[8,64,128]{2,1,0:T(8,128)S(1)}, ...), condition=%wide.region_17.18_spmd.clone, body=%wide.region_15.17_spmd.clone.sunk | while | flops 22689996 | bytes 2389582 | solution.py:76
  98.6 0.9 convolution_add_fusion.11
  107.0 0.9 convolution_add_fusion.11
  115.4 0.9 convolution_add_fusion.11
  126.2 1.5 reshape.687
  127.7 2.9 multiply_reduce_fusion.5
  130.6 8.6 %psum.21 = f32[256]{0:T(256)S(1)} all-reduce(f32[256]{0:T(256)S(1)} %get-tuple-element.392), channel_id=1, replica_groups=mesh['dp'=32,'section'=2,'tensor'=4] {'tensor'}, use_global_device_ids=true, to_apply=%region_19.20 | all-reduce | flops 256 | bytes 2048 | tf_op jit(solution)/shard_map/psum | solution.py:124
  139.2 3.4 convolution_convert_fusion.2
  142.7 2.8 fusion.116
  145.5 18.4 %reduce-scatter.5.cloned.1.call-done = bf16[64,2048]{1,0:T(8,128)(2,1)} async-done(((bf16[256,2048]{1,0:T(8,128)(2,1)}), bf16[64,2048]{1,0:T(8,128)(2,1)}) %reduce-scatter.5.cloned.1.call-update) | async-done | bytes 262160 | tf_op jit(solution)/shard_map/reduce_scatter | solution.py:129
  163.9 1.9 add_convert_fusion.3
  165.9 27.4 %all-gather.4.cloned.1.call-done = bf16[256,2048]{1,0:T(8,128)(2,1)} async-done(((bf16[64,2048]{1,0:T(8,128)(2,1)}), bf16[256,2048]{1,0:T(8,128)(2,1)}) %all-gather.4.cloned.1.call-update) | async-done | bytes 1048592 | tf_op jit(solution)/shard_map/all_gather | solution.py:137
  193.3 2.3 collective-permute-start
  196.3 0.9 collective-permute-done
  197.2 3.0 fusion.154
  202.4 1.0 copy-done.28
  204.4 1.1 reshape_reshape.10
  205.5 1.0 broadcast.415.clone2.1
  206.5 30.9 %while.43 = (s32[]{:T(128)}, f32[8,64,128]{2,1,0:T(8,128)S(1)}, s32[]{:T(128)}, f32[4,64,8,64]{3,2,1,0:T(8,128)}, s32[4,64]{1,0:T(4,128)}, /*index=5*/f32[4,64,8...) while((s32[]{:T(128)}, f32[8,64,128]{2,1,0:T(8,128)S(1)}, ...), condition=%wide.region_24.25_spmd, body=%wide.region_22.24_spmd.sunk | while | flops 22624460 | bytes 2581539 | solution.py:76
  210.3 0.9 constant_dynamic-slice_fusion.12
  218.0 0.9 constant_dynamic-slice_fusion.12
  225.8 0.9 constant_dynamic-slice_fusion.12
  233.5 0.9 constant_dynamic-slice_fusion.12
  237.4 2.3 reshape.692
  239.7 3.0 multiply_reduce_fusion.4
  242.8 9.2 %psum.22 = f32[256]{0:T(256)S(1)} all-reduce(f32[256]{0:T(256)S(1)} %get-tuple-element.394), channel_id=1, replica_groups=mesh['dp'=32,'section'=2,'tensor'=4] {'tensor'}, use_global_device_ids=true, to_apply=%region_26.27 | all-reduce | flops 256 | bytes 2048 | tf_op jit(solution)/shard_map/psum | solution.py:124
  252.0 3.3 convolution_convert_fusion.1
  255.4 24.6 %reduce-scatter.7.cloned.1.call-done = bf16[64,2048]{1,0:T(8,128)(2,1)} async-done(((bf16[256,2048]{1,0:T(8,128)(2,1)}), bf16[64,2048]{1,0:T(8,128)(2,1)}) %reduce-scatter.7.cloned.1.call-update) | async-done | bytes 262160 | tf_op jit(solution)/shard_map/reduce_scatter | solution.py:129
  280.0 1.9 add_convert_fusion.2
  282.0 27.4 %all-gather.6.cloned.1.call-done = bf16[256,2048]{1,0:T(8,128)(2,1)} async-done(((bf16[64,2048]{1,0:T(8,128)(2,1)}), bf16[256,2048]{1,0:T(8,128)(2,1)}) %all-gather.6.cloned.1.call-update) | async-done | bytes 1048592 | tf_op jit(solution)/shard_map/all_gather | solution.py:137
  309.4 2.3 collective-permute-start.1
  311.8 1.5 collective-permute-done.1
  313.3 3.0 fusion.153
  318.5 1.0 copy-done.29
  320.5 1.1 reshape_reshape.11
  321.6 1.0 broadcast.415.clone
  322.6 22.8 %while.44 = (s32[]{:T(128)}, f32[8,64,128]{2,1,0:T(8,128)S(1)}, s32[]{:T(128)}, f32[4,64,8,64]{3,2,1,0:T(8,128)}, s32[4,64]{1,0:T(4,128)S(1)}, /*index=5*/f32[4,...) while((s32[]{:T(128)}, f32[8,64,128]{2,1,0:T(8,128)S(1)}, ...), condition=%wide.region_31.32_spmd, body=%wide.region_29.31_spmd.sunk | while | flops 22624460 | bytes 2582019 | solution.py:76
  325.1 0.9 constant_dynamic-slice_fusion.13
  330.7 0.9 constant_dynamic-slice_fusion.13
  336.4 0.9 constant_dynamic-slice_fusion.13
  342.1 0.9 constant_dynamic-slice_fusion.13
  345.4 1.5 reshape.697
  346.9 2.8 multiply_reduce_fusion.3
  349.8 9.2 %psum.23 = f32[256]{0:T(256)S(1)} all-reduce(f32[256]{0:T(256)S(1)} %get-tuple-element.396), channel_id=1, replica_groups=mesh['dp'=32,'section'=2,'tensor'=4] {'tensor'}, use_global_device_ids=true, to_apply=%region_33.34 | all-reduce | flops 256 | bytes 2048 | tf_op jit(solution)/shard_map/psum | solution.py:124
  359.0 3.3 convolution_convert_fusion
  362.4 24.6 %reduce-scatter.9.cloned.1.call-done = bf16[64,2048]{1,0:T(8,128)(2,1)} async-done(((bf16[256,2048]{1,0:T(8,128)(2,1)}), bf16[64,2048]{1,0:T(8,128)(2,1)}) %reduce-scatter.9.cloned.1.call-update) | async-done | bytes 262160 | tf_op jit(solution)/shard_map/reduce_scatter | solution.py:129
  387.0 1.9 add_convert_fusion.1
  390.9 2.5 add_convert_fusion
  393.6 0.9 copy-done.10
  395.3 1.3 copy-done.1
  396.6 1.3 copy.198
  397.9 18.4 %all-gather.8.cloned.1.call-done = bf16[256,2048]{1,0:T(8,128)(2,1)} async-done(((bf16[64,2048]{1,0:T(8,128)(2,1)}), bf16[256,2048]{1,0:T(8,128)(2,1)}) %all-gather.8.cloned.1.call-update) | async-done | bytes 1048592 | tf_op jit(solution)/shard_map/all_gather | solution.py:137
  416.4 2.6 bitcast_dynamic-update-slice_fusion
  419.0 219.8 %reduce-scatter.11.cloned.1.call-done = bf16[512,64]{0,1:T(8,128)(2,1)} async-done(((bf16[512,2048]{0,1:T(8,128)(2,1)}), bf16[512,64]{0,1:T(8,128)(2,1)}) %reduce-scatter.11.cloned.1.call-update) | async-done | bytes 65552 | tf_op jit(solution)/shard_map/reduce_scatter | solution.py:256
  (407 shorter events, 79.5 us)
Async XLA Ops:
  7.2 381.8 %copy-start = (bf16[1,512,2048]{2,1,0:T(8,128)(2,1)S(1)}, bf16[1,512,2048]{2,1,0:T(8,128)(2,1)}, u32[]{:S(2)}) copy-start(bf16[1,512,2048]{2,1,0:T(8,128)(2,1)} %param.23) | copy-start | bytes 6291460
  15.2 11.9 %copy-start.26 = (f32[1,8]{1,0:T(1,128)S(1)}, f32[1,8]{1,0:T(1,128)}, u32[]{:S(2)}) copy-start(f32[1,8]{1,0:T(1,128)} %param.31) | copy-start | bytes 100
  15.2 12.6 %copy-start.20 = (s32[128]{0:T(128)S(1)}, s32[128]{0:T(128)}, u32[]{:S(2)}) copy-start(s32[128]{0:T(128)} %param.22) | copy-start | bytes 1540
  15.2 12.7 %copy-start.19 = (s32[128]{0:T(128)S(1)}, s32[128]{0:T(128)}, u32[]{:S(2)}) copy-start(s32[128]{0:T(128)} %param.21) | copy-start | bytes 1540
  15.2 17.0 %copy-start.38 = (f32[1,8]{1,0:T(1,128)S(1)}, f32[1,8]{1,0:T(1,128)}, u32[]{:S(2)}) copy-start(f32[1,8]{1,0:T(1,128)} %param.30) | copy-start | bytes 100
  15.2 61.9 %all-to-all-start = ((bf16[32,16,2048]{2,1,0:T(8,128)(2,1)}), bf16[32,16,2048]{2,1,0:T(8,128)(2,1)}, u32[]{:S(2)}, u32[]{:S(2)}) async-start(bf16[32,16,2048]{2,1,0:T(8,128)(2,1)} %bitcast.297), calls=%async_computation | async-start | bytes 4194304 | tf_op jit(solution)/shard_map/all_to_all | solution.py:203
  27.0 57.9 %copy-start.32 = (bf16[1,2048,8]{1,2,0:T(8,128)(2,1)S(1)}, bf16[1,2048,8]{1,2,0:T(8,128)(2,1)}, u32[]{:S(2)}) copy-start(bf16[1,2048,8]{1,2,0:T(8,128)(2,1)} %param.28) | copy-start | bytes 98308
  27.0 57.9 %copy-start.35 = (f32[1,2048]{1,0:T(1,128)S(1)}, f32[1,2048]{1,0:T(1,128)}, u32[]{:S(2)}) copy-start(f32[1,2048]{1,0:T(1,128)} %param.24) | copy-start | bytes 24580
  27.0 57.9 %copy-start.39 = (f32[1,8]{1,0:T(1,128)S(1)}, f32[1,8]{1,0:T(1,128)}, u32[]{:S(2)}) copy-start(f32[1,8]{1,0:T(1,128)} %param.29) | copy-start | bytes 100
  27.0 137.0 %reduce-scatter.5.cloned.1.call-start = ((), (), s32[]{:S(2)}) async-start(), calls=%async_computation.5 | async-start | bytes 1310720 | tf_op jit(solution)/shard_map/reduce_scatter | solution.py:129
  84.8 5.4 copy-start.24
  87.4 2.9 copy-start.2
  87.4 2.9 copy-start.27
  91.1 1.4 copy-start.14
  92.4 4.2 copy-start.17
  97.5 2.7 copy-start.18
  100.8 4.3 copy-start.17
  105.9 2.7 copy-start.18
  109.3 4.3 copy-start.17
  114.4 2.7 copy-start.18
  117.7 4.3 copy-start.17
  122.8 2.7 copy-start.18
  127.7 11.6 %copy-start.11 = (f32[1,512]{1,0:T(1,128)S(1)}, f32[1,512]{1,0:T(1,128)}, u32[]{:S(2)}) copy-start(f32[1,512]{1,0:T(1,128)} %param.32) | copy-start | bytes 6148
  130.5 12.0 %copy-start.5 = (f32[256,512]{1,0:T(8,128)}, f32[256,512]{1,0:T(8,128)S(1)}, u32[]{:S(2)}) copy-start(f32[256,512]{1,0:T(8,128)S(1)} %get-tuple-element.393) | copy-start | bytes 1572868
  139.2 3.4 copy-start.15
  142.6 50.7 %all-gather.4.cloned.1.call-start = ((), (), s32[]{:S(2)}) async-start(), calls=%async_computation.6 | async-start | bytes 1310720 | tf_op jit(solution)/shard_map/all_gather | solution.py:137
  142.7 52.9 %copy-start.22 = (s32[256]{0:T(256)S(1)}, s32[256]{0:T(256)}, u32[]{:S(2)}) copy-start(s32[256]{0:T(256)} %get-tuple-element.388) | copy-start | bytes 3076
  165.9 114.2 %reduce-scatter.7.cloned.1.call-start = ((), (), s32[]{:S(2)}) async-start(), calls=%async_computation.7 | async-start | bytes 1310720 | tf_op jit(solution)/shard_map/reduce_scatter | solution.py:129
  193.3 3.9 collective-permute-start
  196.3 4.3 copy-start.33
  196.3 4.3 copy-start.36
  196.3 4.3 copy-start.40
  200.2 2.2 copy-start.4
  200.2 1.6 copy-start.30
  200.5 1.8 copy-start.25
  201.8 1.6 copy-start.28
  204.2 2.3 copy-start.13
  242.8 12.6 %copy-start.7 = (f32[256,512]{1,0:T(8,128)}, f32[256,512]{1,0:T(8,128)S(1)}, u32[]{:S(2)}) copy-start(f32[256,512]{1,0:T(8,128)S(1)} %get-tuple-element.395) | copy-start | bytes 1572868
  255.3 56.3 %copy-start.21 = (s32[256]{0:T(256)S(1)}, s32[256]{0:T(256)}, u32[]{:S(2)}) copy-start(s32[256]{0:T(256)} %get-tuple-element.387) | copy-start | bytes 3076
  255.4 54.0 %all-gather.6.cloned.1.call-start = ((), (), s32[]{:S(2)}) async-start(), calls=%async_computation.8 | async-start | bytes 1310720 | tf_op jit(solution)/shard_map/all_gather | solution.py:137
  281.9 105.1 %reduce-scatter.9.cloned.1.call-start = ((), (), s32[]{:S(2)}) async-start(), calls=%async_computation.9 | async-start | bytes 1310720 | tf_op jit(solution)/shard_map/reduce_scatter | solution.py:129
  309.4 3.9 collective-permute-start.1
  311.8 4.8 copy-start.34
  311.8 4.8 copy-start.37
  311.8 4.8 copy-start.41
  316.3 2.2 copy-start.3
  316.3 1.6 copy-start.31
  317.9 1.6 copy-start.29
  320.3 2.3 copy-start.12
  322.6 24.3 %copy-start.23 = (f32[512]{0:T(512)S(1)}, f32[512]{0:T(512)}, u32[]{:S(2)}) copy-start(f32[512]{0:T(512)} %mul.547) | copy-start | bytes 6148
  362.3 26.7 %copy-start.6 = (f32[256,512]{1,0:T(8,128)S(1)}, f32[256,512]{1,0:T(8,128)}, u32[]{:S(2)}) copy-start(f32[256,512]{1,0:T(8,128)} %copy-done.5) | copy-start | bytes 1572868
  362.3 26.7 %copy-start.16 = (f32[256]{0:T(256)S(1)}, f32[256]{0:T(256)}, u32[]{:S(2)}) copy-start(f32[256]{0:T(256)} %copy-done.15) | copy-start | bytes 3076
  362.3 54.0 %all-gather.8.cloned.1.call-start = ((), (), s32[]{:S(2)}) async-start(), calls=%async_computation.10 | async-start | bytes 1310720 | tf_op jit(solution)/shard_map/all_gather | solution.py:137
  388.9 249.8 %reduce-scatter.11.cloned.1.call-start = ((), (), s32[]{:S(2)}) async-start(), calls=%async_computation.11 | async-start | bytes 2162688 | tf_op jit(solution)/shard_map/reduce_scatter | solution.py:256
  389.0 1.0 copy-start.8
  393.3 1.2 copy-start.10
  393.4 1.5 copy-start.9
  395.3 1.3 copy-start.1
Sparse Core Ops, SparseCore 0:
  142.7 21.1 reduce-scatter.4
  166.0 27.2 all-gather.3
  255.5 24.5 reduce-scatter.6
  282.0 27.2 all-gather.5
  362.5 24.5 reduce-scatter.8
  389.1 27.2 all-gather.7
  421.2 217.4 reduce-scatter.10
where the time goes:
time: 648 us; the launch traced here: 646 us
  waiting for transfers between devices  408 us (63%)
  local copies, waits for them, and re-layouts  66.8 us (10%)
  matrix products  51.8 us (8%)
  other arithmetic  44.7 us (7%)
  blocking collectives  27 us (4%)
  starting transfers between devices  16.6 us (3%)
  loops' own time  15.7 us (2%)
  between operations  14.8 us (2%)
    reduce_scatter x1, waiting for transfers between devices, per_device(): lax.psum_scatter(grad_acc.astype(jnp.bfloat16), 'dp', scatter_dimension=1...  220 us
    all_gather x3, waiting for transfers between devices, block_layer(): result = lax.all_gather(own_out, 'tensor', axis=0, tiled=True)  73.3 us
    reduce_scatter x3, waiting for transfers between devices, block_layer(): lax.psum_scatter(jnp.dot(y_norm, out_proj, preferred_element_type=jnp.flo...  67.7 us
    all_to_all x1, waiting for transfers between devices, per_device(): lax.all_to_all(outgoing, 'dp', split_axis=0, concat_axis=0, tiled=True)  44.9 us
    psum x3, blocking collectives, block_layer(): sq_sum = lax.psum(jnp.sum(gated * gated, axis=-1), 'tensor')  27 us
    another operation x3, loops' own time, block_scan(): lax.scan(advance, (state, prev_segment), scanned)  15.7 us
  transfers between devices with their start and end apart: 10, of which 10 were waited for; matrix products, arithmetic and copies ran while one was open for 3% of the time, Pallas kernels for 0%

commit v1 on v0

--- a/solution.py
+++ b/solution.py
@@ -134,7 +134,10 @@
     ).astype(jnp.float32)
     own_rows = lax.dynamic_slice_in_dim(rows_f, lax.axis_index("tensor") * row_share, row_share, 0)
     own_out = (own_rows + summed).astype(jnp.bfloat16)
-    result = lax.all_gather(own_out, "tensor", axis=0, tiled=True)
+    size = lax.axis_size("tensor")
+    tiles = jnp.stack([own_out for _ in range(size)])
+    tiles = lax.all_to_all(tiles, "tensor", split_axis=0, concat_axis=0)
+    result = jnp.concatenate(tiles, axis=0)
     return (result, y_norm, (state_end, segment_end))
 
 

time: 648 us -> 600 us (0.926)
  waiting for transfers between devices: 408 us -> 316 us
  blocking collectives: 27 us -> 63.3 us
    all_gather x3 -> x0, waiting for transfers between devices: 73.3 us -> none  [block_layer(): result = lax.all_gather(own_out, 'tensor', axis=0, tiled=True)]
    all_to_all x0 -> x2, blocking collectives: none -> 36.3 us  [block_layer(): tiles = lax.all_to_all(tiles, 'tensor', split_axis=0, concat_axis=0)]
    reduce_scatter x1, waiting for transfers between devices: 220 us -> 199 us  [per_device(): lax.psum_scatter(grad_acc.astype(jnp.bfloat16), 'dp', scatter_dimension=1...]
    all_to_all x0 -> x1, waiting for transfers between devices: none -> 6.62 us  [block_layer(): tiles = lax.all_to_all(tiles, 'tensor', split_axis=0, concat_axis=0)]
  transfers between devices with their start and end apart: 10 -> 8, of which waited for: 10 -> 8; matrix products, arithmetic and copies ran while one was open for 3% -> 4% of each run, Pallas kernels for 0% -> 0%
where the time goes in v1:
time: 600 us; the launch traced here: 597 us
  waiting for transfers between devices  316 us (53%)
  local copies, waits for them, and re-layouts  67.7 us (11%)
  blocking collectives  63.3 us (11%)
  matrix products  51.8 us (9%)
  other arithmetic  45.3 us (8%)
  starting transfers between devices  22.4 us (4%)
  loops' own time  16.7 us (3%)
  between operations  14.5 us (2%)
    reduce_scatter x1, waiting for transfers between devices, per_device(): lax.psum_scatter(grad_acc.astype(jnp.bfloat16), 'dp', scatter_dimension=1...  199 us
    reduce_scatter x3, waiting for transfers between devices, block_layer(): lax.psum_scatter(jnp.dot(y_norm, out_proj, preferred_element_type=jnp.flo...  62.5 us
    all_to_all x1, waiting for transfers between devices, per_device(): lax.all_to_all(outgoing, 'dp', split_axis=0, concat_axis=0, tiled=True)  44.9 us
    all_to_all x2, blocking collectives, block_layer(): tiles = lax.all_to_all(tiles, 'tensor', split_axis=0, concat_axis=0)  36.3 us
    psum x3, blocking collectives, block_layer(): sq_sum = lax.psum(jnp.sum(gated * gated, axis=-1), 'tensor')  27 us
    another operation x3, loops' own time, block_scan(): lax.scan(advance, (state, prev_segment), scanned)  16.7 us
  transfers between devices with their start and end apart: 8, of which 8 were waited for; matrix products, arithmetic and copies ran while one was open for 4% of the time, Pallas kernels for 0%

profile of v1, /device:TPU:2, one launch (start us, length us, event | category | flops | bytes accessed | tf_op | source)
XLA Modules:
  0.0 597.4 jit_solution(10268470663560738328)
XLA Ops:
  7.2 1.0 select_reduce_fusion.3
  10.8 4.4 scatter_custom_fusion
  15.2 11.8 %all-to-all-start = ((bf16[32,16,2048]{2,1,0:T(8,128)(2,1)}), bf16[32,16,2048]{2,1,0:T(8,128)(2,1)}, u32[]{:S(2)}, u32[]{:S(2)}) async-start(bf16[32,16,2048]{2,1,0:T(8,128)(2,1)} %bitcast.301), calls=%async_computation | async-start | bytes 4194304 | tf_op jit(solution)/shard_map/all_to_all | solution.py:206
  28.2 2.4 scatter_custom_fusion.2
  32.2 44.9 %all-to-all-done = bf16[32,16,2048]{2,1,0:T(8,128)(2,1)} async-done(((bf16[32,16,2048]{2,1,0:T(8,128)(2,1)}), bf16[32,16,2048]{2,1,0:T(8,128)(2,1)}, u32[]{:S(2)}, u32[]{:S(2)}) %all-to-all-start) | async-done | bytes 2097184 | tf_op jit(solution)/shard_map/all_to_all | solution.py:206
  77.1 6.1 %scatter_custom_fusion.1 = bf16[512,2048]{1,0:T(8,128)(2,1)} fusion(s32[512]{0:T(512)S(1)} %bitcast.321, bf16[512,2048]{1,0:T(8,128)(2,1)} %bitcast.30, bf16[]{:T(256)} %constant.123.clone.1), kind=kCustom, calls=%fused_computation.184 | custom fusion | bytes 2097664 | tf_op jit(solution)/shard_map/scatter | solution.py:211
  83.2 1.6 multiply_reduce_fusion.2
  84.9 1.7 compare_select_fusion.2
  87.4 2.2 multiply_convert_fusion.20
  91.4 1.1 broadcast.421.clone2
  92.4 32.7 %while.45 = (s32[]{:T(128)}, f32[8,64,128]{2,1,0:T(8,128)S(1)}, s32[]{:T(128)}, f32[4,64,8,64]{3,2,1,0:T(8,128)}, s32[4,64]{1,0:T(4,128)S(1)}, /*index=5*/f32[4,...) while((s32[]{:T(128)}, f32[8,64,128]{2,1,0:T(8,128)S(1)}, ...), condition=%wide.region_17.18_spmd.clone, body=%wide.region_15.17_spmd.clone.sunk | while | flops 22689996 | bytes 2389582 | solution.py:76
  125.2 1.5 reshape.702
  126.7 2.9 multiply_reduce_fusion.5
  129.6 8.6 %psum.21 = f32[256]{0:T(256)S(1)} all-reduce(f32[256]{0:T(256)S(1)} %get-tuple-element.392), channel_id=1, replica_groups=mesh['dp'=32,'section'=2,'tensor'=4] {'tensor'}, use_global_device_ids=true, to_apply=%region_19.20 | all-reduce | flops 256 | bytes 2048 | tf_op jit(solution)/shard_map/psum | solution.py:124
  138.2 3.4 convolution_convert_fusion.2
  141.6 2.8 fusion.116
  144.5 18.5 %reduce-scatter.5.cloned.1.call-done = bf16[64,2048]{1,0:T(8,128)(2,1)} async-done(((bf16[256,2048]{1,0:T(8,128)(2,1)}), bf16[64,2048]{1,0:T(8,128)(2,1)}) %reduce-scatter.5.cloned.1.call-update) | async-done | bytes 262160 | tf_op jit(solution)/shard_map/reduce_scatter | solution.py:129
  163.0 1.2 add_convert_fusion.3
  164.3 18.1 %all_to_all.20 = bf16[4,64,2048]{2,1,0:T(8,128)(2,1)} all-to-all(bf16[4,64,2048]{2,1,0:T(8,128)(2,1)S(1)} %stack.6), channel_id=1, replica_groups=mesh['dp'=32,'section'=2,'tensor'=4] {'tensor'}, dimensions={0} | all-to-all | bytes 2097152 | tf_op jit(solution)/shard_map/all_to_all | solution.py:139
  182.4 2.3 collective-permute-start
  185.4 0.9 collective-permute-done
  186.3 3.0 fusion.154
  191.5 1.0 copy-done.32
  193.5 1.1 reshape_reshape.10
  194.6 1.0 broadcast.421.clone2.1
  195.6 31.7 %while.43 = (s32[]{:T(128)}, f32[8,64,128]{2,1,0:T(8,128)S(1)}, s32[]{:T(128)}, f32[4,64,8,64]{3,2,1,0:T(8,128)}, s32[4,64]{1,0:T(4,128)}, /*index=5*/f32[4,64,8...) while((s32[]{:T(128)}, f32[8,64,128]{2,1,0:T(8,128)S(1)}, ...), condition=%wide.region_24.25_spmd, body=%wide.region_22.24_spmd.sunk | while | flops 22624460 | bytes 2581539 | solution.py:76
  199.6 0.9 constant_dynamic-slice_fusion.12
  207.5 0.9 constant_dynamic-slice_fusion.12
  215.4 0.9 constant_dynamic-slice_fusion.12
  223.4 0.9 constant_dynamic-slice_fusion.12
  227.3 2.3 reshape.708
  229.6 3.0 multiply_reduce_fusion.4
  232.7 9.2 %psum.22 = f32[256]{0:T(256)S(1)} all-reduce(f32[256]{0:T(256)S(1)} %get-tuple-element.394), channel_id=1, replica_groups=mesh['dp'=32,'section'=2,'tensor'=4] {'tensor'}, use_global_device_ids=true, to_apply=%region_26.27 | all-reduce | flops 256 | bytes 2048 | tf_op jit(solution)/shard_map/psum | solution.py:124
  241.9 3.4 convolution_convert_fusion.1
  245.4 24.2 %reduce-scatter.7.cloned.1.call-done = bf16[64,2048]{1,0:T(8,128)(2,1)} async-done(((bf16[256,2048]{1,0:T(8,128)(2,1)}), bf16[64,2048]{1,0:T(8,128)(2,1)}) %reduce-scatter.7.cloned.1.call-update) | async-done | bytes 262160 | tf_op jit(solution)/shard_map/reduce_scatter | solution.py:129
  269.6 1.2 add_convert_fusion.2
  270.9 18.2 %all_to_all.21 = bf16[4,64,2048]{2,1,0:T(8,128)(2,1)} all-to-all(bf16[4,64,2048]{2,1,0:T(8,128)(2,1)S(1)} %stack.7), channel_id=1, replica_groups=mesh['dp'=32,'section'=2,'tensor'=4] {'tensor'}, dimensions={0} | all-to-all | bytes 2097152 | tf_op jit(solution)/shard_map/all_to_all | solution.py:139
  289.1 2.3 collective-permute-start.1
  291.5 1.5 collective-permute-done.1
  293.0 3.0 fusion.153
  298.1 1.0 copy-done.33
  300.2 1.1 reshape_reshape.11
  301.2 1.1 broadcast.421.clone
  302.3 24.7 %while.44 = (s32[]{:T(128)}, f32[8,64,128]{2,1,0:T(8,128)S(1)}, s32[]{:T(128)}, f32[4,64,8,64]{3,2,1,0:T(8,128)}, s32[4,64]{1,0:T(4,128)S(1)}, /*index=5*/f32[4,...) while((s32[]{:T(128)}, f32[8,64,128]{2,1,0:T(8,128)S(1)}, ...), condition=%wide.region_31.32_spmd, body=%wide.region_29.31_spmd.sunk | while | flops 22624460 | bytes 2590267 | solution.py:76
  305.1 0.9 constant_dynamic-slice_fusion.13
  311.3 0.9 constant_dynamic-slice_fusion.13
  317.5 0.9 constant_dynamic-slice_fusion.13
  323.6 0.9 constant_dynamic-slice_fusion.13
  327.0 1.5 reshape.714
  328.5 2.9 multiply_reduce_fusion.3
  331.4 9.2 %psum.23 = f32[256]{0:T(256)S(1)} all-reduce(f32[256]{0:T(256)S(1)} %get-tuple-element.396), channel_id=1, replica_groups=mesh['dp'=32,'section'=2,'tensor'=4] {'tensor'}, use_global_device_ids=true, to_apply=%region_33.34 | all-reduce | flops 256 | bytes 2048 | tf_op jit(solution)/shard_map/psum | solution.py:124
  340.6 3.4 convolution_convert_fusion
  346.0 2.4 add_convert_fusion
  348.4 19.7 %reduce-scatter.9.cloned.1.call-done = bf16[64,2048]{1,0:T(8,128)(2,1)} async-done(((bf16[256,2048]{1,0:T(8,128)(2,1)}), bf16[64,2048]{1,0:T(8,128)(2,1)}) %reduce-scatter.9.cloned.1.call-update) | async-done | bytes 262160 | tf_op jit(solution)/shard_map/reduce_scatter | solution.py:129
  368.1 1.2 add_convert_fusion.1
  369.3 1.1 stack.8
  370.4 5.9 all-to-all-start.3
  376.6 1.5 select_dynamic-update-slice_fusion.1
  378.0 1.6 select_dynamic-update-slice_fusion
  379.7 1.3 copy-done.1
  381.0 1.3 copy.198
  382.3 6.6 %all-to-all-done.3 = bf16[4,64,2048]{2,1,0:T(8,128)(2,1)S(1)} async-done(((bf16[4,64,2048]{2,1,0:T(8,128)(2,1)}), bf16[4,64,2048]{2,1,0:T(8,128)(2,1)S(1)}, u32[]{:S(2)}, u32[]{:S(2)}) %all-to-all-start.3) | async-done | bytes 1048608 | tf_op jit(solution)/shard_map/all_to_all | solution.py:139
  389.0 2.6 bitcast_dynamic-update-slice_fusion
  391.5 199.3 %reduce-scatter.11.cloned.1.call-done = bf16[512,64]{0,1:T(8,128)(2,1)} async-done(((bf16[512,2048]{0,1:T(8,128)(2,1)}), bf16[512,64]{0,1:T(8,128)(2,1)}) %reduce-scatter.11.cloned.1.call-update) | async-done | bytes 65552 | tf_op jit(solution)/shard_map/reduce_scatter | solution.py:259
  (427 shorter events, 82.3 us)
Async XLA Ops:
  7.2 336.9 %copy-start = (bf16[1,512,2048]{2,1,0:T(8,128)(2,1)S(1)}, bf16[1,512,2048]{2,1,0:T(8,128)(2,1)}, u32[]{:S(2)}) copy-start(bf16[1,512,2048]{2,1,0:T(8,128)(2,1)} %param.23) | copy-start | bytes 6291460
  15.2 11.9 %copy-start.30 = (f32[1,8]{1,0:T(1,128)S(1)}, f32[1,8]{1,0:T(1,128)}, u32[]{:S(2)}) copy-start(f32[1,8]{1,0:T(1,128)} %param.31) | copy-start | bytes 100
  15.2 12.6 %copy-start.22 = (s32[128]{0:T(128)S(1)}, s32[128]{0:T(128)}, u32[]{:S(2)}) copy-start(s32[128]{0:T(128)} %param.22) | copy-start | bytes 1540
  15.2 12.7 %copy-start.21 = (s32[128]{0:T(128)S(1)}, s32[128]{0:T(128)}, u32[]{:S(2)}) copy-start(s32[128]{0:T(128)} %param.21) | copy-start | bytes 1540
  15.2 17.0 %copy-start.43 = (f32[1,8]{1,0:T(1,128)S(1)}, f32[1,8]{1,0:T(1,128)}, u32[]{:S(2)}) copy-start(f32[1,8]{1,0:T(1,128)} %param.30) | copy-start | bytes 100
  15.2 61.9 %all-to-all-start = ((bf16[32,16,2048]{2,1,0:T(8,128)(2,1)}), bf16[32,16,2048]{2,1,0:T(8,128)(2,1)}, u32[]{:S(2)}, u32[]{:S(2)}) async-start(bf16[32,16,2048]{2,1,0:T(8,128)(2,1)} %bitcast.301), calls=%async_computation | async-start | bytes 4194304 | tf_op jit(solution)/shard_map/all_to_all | solution.py:206
  27.0 57.9 %copy-start.36 = (bf16[1,2048,8]{1,2,0:T(8,128)(2,1)S(1)}, bf16[1,2048,8]{1,2,0:T(8,128)(2,1)}, u32[]{:S(2)}) copy-start(bf16[1,2048,8]{1,2,0:T(8,128)(2,1)} %param.28) | copy-start | bytes 98308
  27.0 57.9 %copy-start.39 = (f32[1,2048]{1,0:T(1,128)S(1)}, f32[1,2048]{1,0:T(1,128)}, u32[]{:S(2)}) copy-start(f32[1,2048]{1,0:T(1,128)} %param.24) | copy-start | bytes 24580
  27.0 57.9 %copy-start.44 = (f32[1,8]{1,0:T(1,128)S(1)}, f32[1,8]{1,0:T(1,128)}, u32[]{:S(2)}) copy-start(f32[1,8]{1,0:T(1,128)} %param.29) | copy-start | bytes 100
  27.0 136.0 %reduce-scatter.5.cloned.1.call-start = ((), (), s32[]{:S(2)}) async-start(), calls=%async_computation.8 | async-start | bytes 1310720 | tf_op jit(solution)/shard_map/reduce_scatter | solution.py:129
  84.8 5.4 copy-start.28
  87.4 2.9 copy-start.2
  87.4 2.9 copy-start.31
  91.1 1.4 copy-start.12
  92.4 4.1 copy-start.19
  97.3 2.7 copy-start.20
  100.6 4.1 copy-start.19
  105.5 2.7 copy-start.20
  108.8 4.1 copy-start.19
  113.7 2.7 copy-start.20
  117.0 4.1 copy-start.19
  121.9 2.7 copy-start.20
  126.7 11.5 %copy-start.9 = (f32[1,512]{1,0:T(1,128)S(1)}, f32[1,512]{1,0:T(1,128)}, u32[]{:S(2)}) copy-start(f32[1,512]{1,0:T(1,128)} %param.32) | copy-start | bytes 6148
  129.5 12.0 %copy-start.5 = (f32[256,512]{1,0:T(8,128)}, f32[256,512]{1,0:T(8,128)S(1)}, u32[]{:S(2)}) copy-start(f32[256,512]{1,0:T(8,128)S(1)} %get-tuple-element.393) | copy-start | bytes 1572868
  138.2 3.4 copy-start.13
  141.6 128.0 %reduce-scatter.7.cloned.1.call-start = ((), (), s32[]{:S(2)}) async-start(), calls=%async_computation.9 | async-start | bytes 1310720 | tf_op jit(solution)/shard_map/reduce_scatter | solution.py:129
  144.5 40.2 %copy-start.24 = (s32[256]{0:T(256)S(1)}, s32[256]{0:T(256)}, u32[]{:S(2)}) copy-start(s32[256]{0:T(256)} %get-tuple-element.388) | copy-start | bytes 3076
  182.4 3.9 collective-permute-start
  185.3 4.3 copy-start.37
  185.3 4.3 copy-start.40
  185.4 4.2 copy-start.45
  189.3 2.2 copy-start.4
  189.3 1.6 copy-start.34
  189.6 1.8 copy-start.29
  190.9 1.6 copy-start.32
  193.3 2.3 copy-start.11
  232.7 12.6 %copy-start.7 = (f32[256,512]{1,0:T(8,128)}, f32[256,512]{1,0:T(8,128)S(1)}, u32[]{:S(2)}) copy-start(f32[256,512]{1,0:T(8,128)S(1)} %get-tuple-element.395) | copy-start | bytes 1572868
  241.9 3.4 copy-start.15
  245.3 122.8 %reduce-scatter.9.cloned.1.call-start = ((), (), s32[]{:S(2)}) async-start(), calls=%async_computation.10 | async-start | bytes 1310720 | tf_op jit(solution)/shard_map/reduce_scatter | solution.py:129
  269.6 21.8 %copy-start.23 = (s32[256]{0:T(256)S(1)}, s32[256]{0:T(256)}, u32[]{:S(2)}) copy-start(s32[256]{0:T(256)} %get-tuple-element.387) | copy-start | bytes 3076
  289.1 3.9 collective-permute-start.1
  291.4 4.8 copy-start.38
  291.5 4.8 copy-start.41
  291.5 4.8 copy-start.46
  296.0 2.2 copy-start.3
  296.0 1.6 copy-start.35
  296.3 1.8 copy-start.26
  297.6 1.6 copy-start.33
  300.0 2.3 copy-start.10
  302.3 26.2 %copy-start.25 = (f32[512]{0:T(512)S(1)}, f32[512]{0:T(512)}, u32[]{:S(2)}) copy-start(f32[512]{0:T(512)} %mul.547) | copy-start | bytes 6148
  302.3 26.2 %copy-start.27 = (f32[256]{0:T(256)S(1)}, f32[256]{0:T(256)}, u32[]{:S(2)}) copy-start(f32[256]{0:T(256)} %copy-done.26) | copy-start | bytes 3076
  302.3 26.2 %copy-start.42 = (f32[1,2048]{1,0:T(1,128)S(1)}, f32[1,2048]{1,0:T(1,128)}, u32[]{:S(2)}) copy-start(f32[1,2048]{1,0:T(1,128)} %param.24) | copy-start | bytes 24580
  302.3 2.4 copy-start.17
  306.5 1.3 copy-start.18
  308.5 2.4 copy-start.17
  312.7 1.3 copy-start.18
  314.7 2.4 copy-start.17
  320.8 2.4 copy-start.17
  325.0 1.3 copy-start.18
  340.6 3.5 copy-start.6
  340.6 3.5 copy-start.14
  344.0 246.8 %reduce-scatter.11.cloned.1.call-start = ((), (), s32[]{:S(2)}) async-start(), calls=%async_computation.11 | async-start | bytes 2162688 | tf_op jit(solution)/shard_map/reduce_scatter | solution.py:259
  370.4 18.5 %all-to-all-start.3 = ((bf16[4,64,2048]{2,1,0:T(8,128)(2,1)}), bf16[4,64,2048]{2,1,0:T(8,128)(2,1)S(1)}, u32[]{:S(2)}, u32[]{:S(2)}) async-start(bf16[4,64,2048]{2,1,0:T(8,128)(2,1)} %stack.8), calls=%async_computation.6 | async-start | bytes 2097152 | tf_op jit(solution)/shard_map/all_to_all | solution.py:139
  379.7 1.4 copy-start.1
  (3 other events, 3.4 us)
Sparse Core Ops, SparseCore 0:
  141.7 21.2 reduce-scatter.4
  245.4 24.1 reduce-scatter.6
  344.1 23.9 reduce-scatter.8
  372.9 217.9 reduce-scatter.10
